TPU v7x, 256 devices: a whole 4x4x8 slice. The times are simulated.
256 devices in a mesh: seq: 32 (over y, z), head: 8 (over x, core).
Axes of the slice: x: 4, y: 4, z: 8, core: 2. Of those that a mesh axis runs over, the one named last changes fastest.
Arguments:
- tokens: bfloat16 [32768, 4096], P('seq'), may hold values from -50 to 50
- norm_gain: float32 [4096], replicated, may hold values from 0.1 to 1.9
- wq: bfloat16 [4096, 4096], P('seq', 'head'), may hold values from -2.34375 to 2.34375
- wk: bfloat16 [4096, 1024], P('seq', 'head'), may hold values from -0.09375 to 0.09375
- wv: bfloat16 [4096, 1024], P('seq', 'head'), may hold values from -0.09375 to 0.09375
- wo: bfloat16 [4096, 4096], P('head', 'seq'), may hold values from -0.1875 to 0.1875
- gate_bias: float32 [32], P('head'), may hold values from -3 to 3
- mem_init: float32 [8, 128, 128], P('head'), may hold values from -32768 to 32768
- norm_init: float32 [8, 128], P('head'), may hold values from 512 to 2048
Outputs:
- attended: bfloat16 [32768, 4096], P('seq', 'head')
All inputs are finite; a program needn't handle non-finite values.
Results may differ from a plain program's by a relative error of at most 0.018.
Values may be sent and summed in bfloat16 or wider, within the bound.
No kernel may reach another device: no remote copies, remote signals or barrier semaphores. Data moves between devices by JAX's collectives and lax.ppermute only.
A program may use at most 128 MiB of HBM per device.

v0:
```python
import math
import jax
import jax.numpy as jnp
from jax import lax
from jax.sharding import PartitionSpec as P

H = 32
KVH = 8
HD = 128
SEG = 512


def from_behind(block, axis, distance):
    devices = range(lax.axis_size(axis))
    route = [(i - distance, i) for i in devices if i - distance in devices]
    return lax.ppermute(block, axis, route)


def feature_map(values_in):
    return jnp.where(values_in > 0, values_in + 1.0, jnp.exp(jnp.minimum(values_in, 0.0)))


def per_device(tokens, norm_gain, wq, wk, wv, wo, gate_bias, mem_init, norm_init):
    highest = lax.Precision.HIGHEST
    widened = tokens.astype(jnp.float32)
    normed = (
        widened * lax.rsqrt(jnp.mean(widened * widened, axis=-1, keepdims=True) + 1e-05) * norm_gain
    ).astype(jnp.bfloat16)
    token_count = normed.shape[0]

    def project(shard_piece):
        return jnp.dot(normed, shard_piece, preferred_element_type=jnp.float32)

    query_wide = project(lax.all_gather(wq, "seq", axis=0, tiled=True))
    key_wide = project(lax.all_gather(wk, "seq", axis=0, tiled=True))
    value_wide = project(lax.all_gather(wv, "seq", axis=0, tiled=True))
    queries = query_wide.astype(jnp.bfloat16)
    keys_all = key_wide.astype(jnp.bfloat16)
    values_all = value_wide.astype(jnp.bfloat16)
    group = H // KVH
    kv_local = wk.shape[1] // HD
    segments = token_count // SEG
    query_seg = queries.reshape(segments, SEG, kv_local, group, HD)
    key_seg = keys_all.reshape(segments, SEG, kv_local, HD)
    value_seg = values_all.reshape(segments, SEG, kv_local, HD)
    key_feats = feature_map(key_seg.astype(jnp.float32))
    delta_mem = jnp.einsum(
        "nski,nskj->nkij", key_feats, value_seg.astype(jnp.float32), precision=highest
    )
    delta_norm = jnp.sum(key_feats, axis=1)
    own_mem = jnp.sum(delta_mem, axis=0)
    own_norm = jnp.sum(delta_norm, axis=0)
    zero_mem = jnp.zeros_like(own_mem)
    zero_norm = jnp.zeros_like(own_norm)

    def pass_along(step_index, carried):
        return (
            from_behind((carried[0] + own_mem).astype(jnp.bfloat16), "seq", 1).astype(jnp.float32),
            from_behind((carried[1] + own_norm).astype(jnp.bfloat16), "seq", 1).astype(jnp.float32),
        )

    carried_mem, carried_norm = lax.fori_loop(
        0, lax.axis_size("seq") - 1, pass_along, (zero_mem, zero_norm)
    )
    inner_mem = jnp.concatenate([zero_mem[None], jnp.cumsum(delta_mem, axis=0)[:-1]], axis=0)
    inner_norm = jnp.concatenate([zero_norm[None], jnp.cumsum(delta_norm, axis=0)[:-1]], axis=0)
    mem_before = mem_init[None] + carried_mem[None] + inner_mem
    norm_before = norm_init[None] + carried_norm[None] + inner_norm
    query_feats = feature_map(query_seg.astype(jnp.float32))
    numer = jnp.einsum("nskgi,nkij->nskgj", query_feats, mem_before, precision=highest)
    denom = jnp.einsum("nskgi,nki->nskg", query_feats, norm_before, precision=highest)
    retrieved = numer / denom[..., None]
    score_scale = 1.0 / math.sqrt(HD)
    causal = lax.broadcasted_iota(jnp.int32, (SEG, SEG), 0) >= lax.broadcasted_iota(
        jnp.int32, (SEG, SEG), 1
    )
    scores = (
        jnp.einsum("nqkgd,nskd->nkgqs", query_seg, key_seg, preferred_element_type=jnp.float32)
        * score_scale
    )
    scores = jnp.where(causal, scores, -1e30)
    peak = jnp.max(scores, axis=-1, keepdims=True)
    expd = jnp.exp(scores - peak)
    probs = (expd / jnp.sum(expd, axis=-1, keepdims=True)).astype(jnp.bfloat16)
    local = jnp.einsum("nkgqs,nskd->nqkgd", probs, value_seg, preferred_element_type=jnp.float32)
    gate_mix = jax.nn.sigmoid(gate_bias).reshape(kv_local, group)
    mixed = (
        gate_mix[None, None, :, :, None] * retrieved
        + (1.0 - gate_mix)[None, None, :, :, None] * local
    )
    mixed = mixed.astype(jnp.bfloat16).reshape(token_count, kv_local * group * HD)
    partial_out = jnp.dot(
        mixed, lax.all_gather(wo, "seq", axis=1, tiled=True), preferred_element_type=jnp.float32
    )
    return lax.psum_scatter(
        partial_out.astype(jnp.bfloat16), "head", scatter_dimension=1, tiled=True
    )


def solution(mesh):
    placed = (
        P("seq", None),
        P(),
        P("seq", "head"),
        P("seq", "head"),
        P("seq", "head"),
        P("head", "seq"),
        P("head"),
        P("head", None, None),
        P("head", None),
    )
    return jax.shard_map(
        per_device, mesh=mesh, in_specs=placed, out_specs=P("seq", "head"), check_vma=False
    )
```

profile of v0, /device:TPU:1, one launch (start us, length us, event | category | flops | bytes accessed | tf_op | source)
XLA Modules:
  0.0 559.1 jit_solution(2536971388080526449)
XLA Ops:
  9.5 5.1 fusion.3
  15.2 10.3 %fusion.5 = bf16[1024,4096]{1,0:T(8,128)(2,1)} fusion(bf16[1024,4096]{1,0:T(8,128)(2,1)} %param.11, f32[4096]{0:T(1024)S(1)} %copy-done.2, f32[1024]{0:T(1024)S(1)} %add_rsqrt_fusion), kind=kLoop, calls=%fused_computation.9 | loop fusion | flops 16777216 | bytes 16797696 | tf_op jit(solution)/shard_map/convert_element_type | solution.py:28
  25.5 60.1 %all-gather.5.cloned.1.call-done = bf16[4096,128]{1,0:T(8,128)(2,1)} async-done(((bf16[128,128]{1,0:T(8,128)(2,1)}), bf16[4096,128]{1,0:T(8,128)(2,1)}) %all-gather.5.cloned.1.call-update) | async-done | bytes 1048592 | tf_op jit(solution)/shard_map/all_gather | solution.py:35
  85.6 6.0 %fusion.38 = (f32[128]{0:T(128)S(1)}, bf16[1024,128]{1,0:T(8,128)(2,1)S(1)}) fusion(bf16[1024,4096]{1,0:T(8,128)(2,1)} %fusion.5, bf16[4096,128]{1,0:T(8,128)(2,1)} %all-gather.5.cloned.1.call-done), kind=kOutput, calls=%fused_computation.57 | convolution fusion | flops 1074659200 | bytes 9699840 | tf_op jit(solution)/shard_map/dot_general | solution.py:32
  91.7 70.3 %all-gather.7.cloned.1.call-done = bf16[4096,128]{1,0:T(8,128)(2,1)} async-done(((bf16[128,128]{1,0:T(8,128)(2,1)}), bf16[4096,128]{1,0:T(8,128)(2,1)}) %all-gather.7.cloned.1.call-update) | async-done | bytes 1048592 | tf_op jit(solution)/shard_map/all_gather | solution.py:36
  162.0 5.9 %convolution_convert_fusion.2 = bf16[1024,128]{1,0:T(8,128)(2,1)S(1)} fusion(bf16[1024,4096]{1,0:T(8,128)(2,1)} %fusion.5, bf16[4096,128]{1,0:T(8,128)(2,1)} %all-gather.7.cloned.1.call-done), kind=kOutput, calls=%fused_computation.32 | convolution fusion | flops 1073872896 | bytes 9699328 | tf_op jit(solution)/shard_map/dot_general | solution.py:32
  168.9 253.9 %while.13 = (s32[]{:T(128)}, f32[1,128,128]{2,1,0:T(8,128)S(1)}, f32[1,128]{1,0:T(1,128)S(1)}, f32[1,128,128]{2,1,0:T(8,128)S(1)}, f32[1,128]{1,0:T(1,128)S(1)}, /*index=5*/s32[]{:T(128)}, s32[]{:T(128)}) while((s32[]{:T(128)}, f32[1,128,128]{2,1,0:T(8,128)S(1)}, f32[1,128]{1,0:T(1,128)S(1)}, f32[1,128,128]{2,1,0:T(8,128)S(1)}, ...), condition=%wide.region_4.5_spmd.clone, body=%wide.region_3.4_spmd.clone.sunk | while | flops 66051 | bytes 396456 | solution.py:62
  171.1 4.0 collective-permute-start.1
  182.2 4.0 collective-permute-start
  190.3 4.0 collective-permute-start
  197.8 4.0 collective-permute-start
  213.7 3.8 collective-permute-start
  221.2 4.0 collective-permute-start
  225.2 3.8 collective-permute-start.1
  229.8 4.0 collective-permute-start
  233.8 4.0 collective-permute-start.1
  238.5 4.0 collective-permute-start
  242.5 3.6 collective-permute-start.1
  246.9 4.0 collective-permute-start
  255.2 3.7 collective-permute-start
  258.9 4.0 collective-permute-start.1
  263.6 3.7 collective-permute-start
  267.4 3.8 collective-permute-start.1
  279.8 4.0 collective-permute-start
  283.8 3.9 collective-permute-start.1
  288.5 3.7 collective-permute-start
  292.2 4.0 collective-permute-start.1
  300.6 3.7 collective-permute-start.1
  305.1 4.0 collective-permute-start
  309.1 3.7 collective-permute-start.1
  313.5 4.0 collective-permute-start
  317.5 4.1 collective-permute-start.1
  322.4 4.0 collective-permute-start
  326.4 3.6 collective-permute-start.1
  330.8 4.0 collective-permute-start
  334.8 4.4 collective-permute-start.1
  340.0 4.0 collective-permute-start
  359.7 3.7 collective-permute-start.1
  367.7 4.3 collective-permute-start.1
  372.8 3.9 collective-permute-start
  384.6 4.1 collective-permute-start.1
  393.1 3.9 collective-permute-start.1
  401.3 4.0 collective-permute-start.1
  409.7 4.0 collective-permute-start.1
  418.1 4.0 collective-permute-start.1
  422.9 9.0 %convolution_convert_fusion.1 = bf16[1024,512]{1,0:T(8,128)(2,1)S(1)} fusion(bf16[1024,4096]{1,0:T(8,128)(2,1)} %fusion.5, bf16[4096,512]{1,0:T(8,128)(2,1)} %all-gather.9.cloned.1.call-done), kind=kOutput, calls=%fused_computation.31 | convolution fusion | flops 4295491584 | bytes 13631488 | tf_op jit(solution)/shard_map/dot_general | solution.py:32
  445.5 8.9 %convolution_convert_fusion = bf16[1024,4096]{1,0:T(8,128)(2,1)} fusion(bf16[512,4096]{1,0:T(8,128)(2,1)} %all-gather.11.cloned.1.call-done, bf16[128,8,4,128]{3,2,1,0:T(4,128)(2,1)S(1)} %bitcast.93), kind=kOutput, calls=%fused_computation.13 | convolution fusion | flops 4299161600 | bytes 13631488 | tf_op jit(solution)/shard_map/dot_general | solution.py:92
  454.5 98.1 %reduce-scatter.2.cloned.1.call-done = bf16[1024,512]{1,0:T(8,128)(2,1)} async-done(((bf16[1024,4096]{1,0:T(8,128)(2,1)}), bf16[1024,512]{1,0:T(8,128)(2,1)}) %reduce-scatter.2.cloned.1.call-update) | async-done | bytes 1048592 | tf_op jit(solution)/shard_map/reduce_scatter | solution.py:95
  (261 shorter events, 121.4 us)
Async XLA Ops:
  6.5 79.0 %all-gather.5.cloned.1.call-start = ((), (), s32[]{:S(2)}) async-start(), calls=%async_computation.1 | async-start | bytes 1081344 | tf_op jit(solution)/shard_map/all_gather | solution.py:35
  7.3 154.7 %all-gather.7.cloned.1.call-start = ((), (), s32[]{:S(2)}) async-start(), calls=%async_computation.2 | async-start | bytes 1081344 | tf_op jit(solution)/shard_map/all_gather | solution.py:36
  8.0 414.9 %all-gather.9.cloned.1.call-start = ((), (), s32[]{:S(2)}) async-start(), calls=%async_computation.3 | async-start | bytes 4325376 | tf_op jit(solution)/shard_map/all_gather | solution.py:34
  8.7 436.8 %all-gather.11.cloned.1.call-start = ((), (), s32[]{:S(2)}) async-start(), calls=%async_computation.4 | async-start | bytes 4325376 | tf_op jit(solution)/shard_map/all_gather | solution.py:93
  9.3 543.3 %reduce-scatter.2.cloned.1.call-start = ((), (), s32[]{:S(2)}) async-start(), calls=%async_computation.5 | async-start | bytes 9437184 | tf_op jit(solution)/shard_map/reduce_scatter | solution.py:95
  168.9 6.9 %collective-permute-start = (bf16[1,128,128]{2,1,0:T(8,128)(2,1)S(1)}, bf16[1,128,128]{2,1,0:T(8,128)(2,1)S(1)}, u32[]{:S(2)}, u32[]{:S(2)}) collective-permute-start(bf16[1,128,128]{2,1,0:T(8,128)(2,1)S(1)} %fusion.74), channel_id=1, source_target_pairs={{0,8},{8,16},{16,24},{24,32},{32,40},{40,48},{48,56},{56,64},{64,7... | collective-permute-start | bytes 98312 | tf_op jit(solution)/shard_map/while/body/eval_jaxpr/ppermute | solution.py:16
  171.1 4.7 collective-permute-start.1
  175.9 6.2 %collective-permute-start = (bf16[1,128,128]{2,1,0:T(8,128)(2,1)S(1)}, bf16[1,128,128]{2,1,0:T(8,128)(2,1)S(1)}, u32[]{:S(2)}, u32[]{:S(2)}) collective-permute-start(bf16[1,128,128]{2,1,0:T(8,128)(2,1)S(1)} %fusion.74), channel_id=1, source_target_pairs={{0,8},{8,16},{16,24},{24,32},{32,40},{40,48},{48,56},{56,64},{64,7... | collective-permute-start | bytes 98312 | tf_op jit(solution)/shard_map/while/body/eval_jaxpr/ppermute | solution.py:16
  182.2 8.1 %collective-permute-start = (bf16[1,128,128]{2,1,0:T(8,128)(2,1)S(1)}, bf16[1,128,128]{2,1,0:T(8,128)(2,1)S(1)}, u32[]{:S(2)}, u32[]{:S(2)}) collective-permute-start(bf16[1,128,128]{2,1,0:T(8,128)(2,1)S(1)} %fusion.74), channel_id=1, source_target_pairs={{0,8},{8,16},{16,24},{24,32},{32,40},{40,48},{48,56},{56,64},{64,7... | collective-permute-start | bytes 98312 | tf_op jit(solution)/shard_map/while/body/eval_jaxpr/ppermute | solution.py:16
  190.3 7.4 %collective-permute-start = (bf16[1,128,128]{2,1,0:T(8,128)(2,1)S(1)}, bf16[1,128,128]{2,1,0:T(8,128)(2,1)S(1)}, u32[]{:S(2)}, u32[]{:S(2)}) collective-permute-start(bf16[1,128,128]{2,1,0:T(8,128)(2,1)S(1)} %fusion.74), channel_id=1, source_target_pairs={{0,8},{8,16},{16,24},{24,32},{32,40},{40,48},{48,56},{56,64},{64,7... | collective-permute-start | bytes 98312 | tf_op jit(solution)/shard_map/while/body/eval_jaxpr/ppermute | solution.py:16
  197.8 8.1 %collective-permute-start = (bf16[1,128,128]{2,1,0:T(8,128)(2,1)S(1)}, bf16[1,128,128]{2,1,0:T(8,128)(2,1)S(1)}, u32[]{:S(2)}, u32[]{:S(2)}) collective-permute-start(bf16[1,128,128]{2,1,0:T(8,128)(2,1)S(1)} %fusion.74), channel_id=1, source_target_pairs={{0,8},{8,16},{16,24},{24,32},{32,40},{40,48},{48,56},{56,64},{64,7... | collective-permute-start | bytes 98312 | tf_op jit(solution)/shard_map/while/body/eval_jaxpr/ppermute | solution.py:16
  205.9 7.8 %collective-permute-start = (bf16[1,128,128]{2,1,0:T(8,128)(2,1)S(1)}, bf16[1,128,128]{2,1,0:T(8,128)(2,1)S(1)}, u32[]{:S(2)}, u32[]{:S(2)}) collective-permute-start(bf16[1,128,128]{2,1,0:T(8,128)(2,1)S(1)} %fusion.74), channel_id=1, source_target_pairs={{0,8},{8,16},{16,24},{24,32},{32,40},{40,48},{48,56},{56,64},{64,7... | collective-permute-start | bytes 98312 | tf_op jit(solution)/shard_map/while/body/eval_jaxpr/ppermute | solution.py:16
  213.7 7.4 %collective-permute-start = (bf16[1,128,128]{2,1,0:T(8,128)(2,1)S(1)}, bf16[1,128,128]{2,1,0:T(8,128)(2,1)S(1)}, u32[]{:S(2)}, u32[]{:S(2)}) collective-permute-start(bf16[1,128,128]{2,1,0:T(8,128)(2,1)S(1)} %fusion.74), channel_id=1, source_target_pairs={{0,8},{8,16},{16,24},{24,32},{32,40},{40,48},{48,56},{56,64},{64,7... | collective-permute-start | bytes 98312 | tf_op jit(solution)/shard_map/while/body/eval_jaxpr/ppermute | solution.py:16
  221.2 8.5 %collective-permute-start = (bf16[1,128,128]{2,1,0:T(8,128)(2,1)S(1)}, bf16[1,128,128]{2,1,0:T(8,128)(2,1)S(1)}, u32[]{:S(2)}, u32[]{:S(2)}) collective-permute-start(bf16[1,128,128]{2,1,0:T(8,128)(2,1)S(1)} %fusion.74), channel_id=1, source_target_pairs={{0,8},{8,16},{16,24},{24,32},{32,40},{40,48},{48,56},{56,64},{64,7... | collective-permute-start | bytes 98312 | tf_op jit(solution)/shard_map/while/body/eval_jaxpr/ppermute | solution.py:16
  229.8 8.7 %collective-permute-start = (bf16[1,128,128]{2,1,0:T(8,128)(2,1)S(1)}, bf16[1,128,128]{2,1,0:T(8,128)(2,1)S(1)}, u32[]{:S(2)}, u32[]{:S(2)}) collective-permute-start(bf16[1,128,128]{2,1,0:T(8,128)(2,1)S(1)} %fusion.74), channel_id=1, source_target_pairs={{0,8},{8,16},{16,24},{24,32},{32,40},{40,48},{48,56},{56,64},{64,7... | collective-permute-start | bytes 98312 | tf_op jit(solution)/shard_map/while/body/eval_jaxpr/ppermute | solution.py:16
  233.8 4.7 collective-permute-start.1
  238.5 8.3 %collective-permute-start = (bf16[1,128,128]{2,1,0:T(8,128)(2,1)S(1)}, bf16[1,128,128]{2,1,0:T(8,128)(2,1)S(1)}, u32[]{:S(2)}, u32[]{:S(2)}) collective-permute-start(bf16[1,128,128]{2,1,0:T(8,128)(2,1)S(1)} %fusion.74), channel_id=1, source_target_pairs={{0,8},{8,16},{16,24},{24,32},{32,40},{40,48},{48,56},{56,64},{64,7... | collective-permute-start | bytes 98312 | tf_op jit(solution)/shard_map/while/body/eval_jaxpr/ppermute | solution.py:16
  246.9 8.3 %collective-permute-start = (bf16[1,128,128]{2,1,0:T(8,128)(2,1)S(1)}, bf16[1,128,128]{2,1,0:T(8,128)(2,1)S(1)}, u32[]{:S(2)}, u32[]{:S(2)}) collective-permute-start(bf16[1,128,128]{2,1,0:T(8,128)(2,1)S(1)} %fusion.74), channel_id=1, source_target_pairs={{0,8},{8,16},{16,24},{24,32},{32,40},{40,48},{48,56},{56,64},{64,7... | collective-permute-start | bytes 98312 | tf_op jit(solution)/shard_map/while/body/eval_jaxpr/ppermute | solution.py:16
  255.2 8.3 %collective-permute-start = (bf16[1,128,128]{2,1,0:T(8,128)(2,1)S(1)}, bf16[1,128,128]{2,1,0:T(8,128)(2,1)S(1)}, u32[]{:S(2)}, u32[]{:S(2)}) collective-permute-start(bf16[1,128,128]{2,1,0:T(8,128)(2,1)S(1)} %fusion.74), channel_id=1, source_target_pairs={{0,8},{8,16},{16,24},{24,32},{32,40},{40,48},{48,56},{56,64},{64,7... | collective-permute-start | bytes 98312 | tf_op jit(solution)/shard_map/while/body/eval_jaxpr/ppermute | solution.py:16
  258.9 4.7 collective-permute-start.1
  263.6 8.3 %collective-permute-start = (bf16[1,128,128]{2,1,0:T(8,128)(2,1)S(1)}, bf16[1,128,128]{2,1,0:T(8,128)(2,1)S(1)}, u32[]{:S(2)}, u32[]{:S(2)}) collective-permute-start(bf16[1,128,128]{2,1,0:T(8,128)(2,1)S(1)} %fusion.74), channel_id=1, source_target_pairs={{0,8},{8,16},{16,24},{24,32},{32,40},{40,48},{48,56},{56,64},{64,7... | collective-permute-start | bytes 98312 | tf_op jit(solution)/shard_map/while/body/eval_jaxpr/ppermute | solution.py:16
  271.9 7.8 %collective-permute-start = (bf16[1,128,128]{2,1,0:T(8,128)(2,1)S(1)}, bf16[1,128,128]{2,1,0:T(8,128)(2,1)S(1)}, u32[]{:S(2)}, u32[]{:S(2)}) collective-permute-start(bf16[1,128,128]{2,1,0:T(8,128)(2,1)S(1)} %fusion.74), channel_id=1, source_target_pairs={{0,8},{8,16},{16,24},{24,32},{32,40},{40,48},{48,56},{56,64},{64,7... | collective-permute-start | bytes 98312 | tf_op jit(solution)/shard_map/while/body/eval_jaxpr/ppermute | solution.py:16
  279.8 8.6 %collective-permute-start = (bf16[1,128,128]{2,1,0:T(8,128)(2,1)S(1)}, bf16[1,128,128]{2,1,0:T(8,128)(2,1)S(1)}, u32[]{:S(2)}, u32[]{:S(2)}) collective-permute-start(bf16[1,128,128]{2,1,0:T(8,128)(2,1)S(1)} %fusion.74), channel_id=1, source_target_pairs={{0,8},{8,16},{16,24},{24,32},{32,40},{40,48},{48,56},{56,64},{64,7... | collective-permute-start | bytes 98312 | tf_op jit(solution)/shard_map/while/body/eval_jaxpr/ppermute | solution.py:16
  283.8 4.6 collective-permute-start.1
  288.5 8.5 %collective-permute-start = (bf16[1,128,128]{2,1,0:T(8,128)(2,1)S(1)}, bf16[1,128,128]{2,1,0:T(8,128)(2,1)S(1)}, u32[]{:S(2)}, u32[]{:S(2)}) collective-permute-start(bf16[1,128,128]{2,1,0:T(8,128)(2,1)S(1)} %fusion.74), channel_id=1, source_target_pairs={{0,8},{8,16},{16,24},{24,32},{32,40},{40,48},{48,56},{56,64},{64,7... | collective-permute-start | bytes 98312 | tf_op jit(solution)/shard_map/while/body/eval_jaxpr/ppermute | solution.py:16
  292.2 4.7 collective-permute-start.1
  297.0 8.0 %collective-permute-start = (bf16[1,128,128]{2,1,0:T(8,128)(2,1)S(1)}, bf16[1,128,128]{2,1,0:T(8,128)(2,1)S(1)}, u32[]{:S(2)}, u32[]{:S(2)}) collective-permute-start(bf16[1,128,128]{2,1,0:T(8,128)(2,1)S(1)} %fusion.74), channel_id=1, source_target_pairs={{0,8},{8,16},{16,24},{24,32},{32,40},{40,48},{48,56},{56,64},{64,7... | collective-permute-start | bytes 98312 | tf_op jit(solution)/shard_map/while/body/eval_jaxpr/ppermute | solution.py:16
  305.1 8.4 %collective-permute-start = (bf16[1,128,128]{2,1,0:T(8,128)(2,1)S(1)}, bf16[1,128,128]{2,1,0:T(8,128)(2,1)S(1)}, u32[]{:S(2)}, u32[]{:S(2)}) collective-permute-start(bf16[1,128,128]{2,1,0:T(8,128)(2,1)S(1)} %fusion.74), channel_id=1, source_target_pairs={{0,8},{8,16},{16,24},{24,32},{32,40},{40,48},{48,56},{56,64},{64,7... | collective-permute-start | bytes 98312 | tf_op jit(solution)/shard_map/while/body/eval_jaxpr/ppermute | solution.py:16
  313.5 8.8 %collective-permute-start = (bf16[1,128,128]{2,1,0:T(8,128)(2,1)S(1)}, bf16[1,128,128]{2,1,0:T(8,128)(2,1)S(1)}, u32[]{:S(2)}, u32[]{:S(2)}) collective-permute-start(bf16[1,128,128]{2,1,0:T(8,128)(2,1)S(1)} %fusion.74), channel_id=1, source_target_pairs={{0,8},{8,16},{16,24},{24,32},{32,40},{40,48},{48,56},{56,64},{64,7... | collective-permute-start | bytes 98312 | tf_op jit(solution)/shard_map/while/body/eval_jaxpr/ppermute | solution.py:16
  317.5 4.8 collective-permute-start.1
  322.4 8.4 %collective-permute-start = (bf16[1,128,128]{2,1,0:T(8,128)(2,1)S(1)}, bf16[1,128,128]{2,1,0:T(8,128)(2,1)S(1)}, u32[]{:S(2)}, u32[]{:S(2)}) collective-permute-start(bf16[1,128,128]{2,1,0:T(8,128)(2,1)S(1)} %fusion.74), channel_id=1, source_target_pairs={{0,8},{8,16},{16,24},{24,32},{32,40},{40,48},{48,56},{56,64},{64,7... | collective-permute-start | bytes 98312 | tf_op jit(solution)/shard_map/while/body/eval_jaxpr/ppermute | solution.py:16
  330.8 9.1 %collective-permute-start = (bf16[1,128,128]{2,1,0:T(8,128)(2,1)S(1)}, bf16[1,128,128]{2,1,0:T(8,128)(2,1)S(1)}, u32[]{:S(2)}, u32[]{:S(2)}) collective-permute-start(bf16[1,128,128]{2,1,0:T(8,128)(2,1)S(1)} %fusion.74), channel_id=1, source_target_pairs={{0,8},{8,16},{16,24},{24,32},{32,40},{40,48},{48,56},{56,64},{64,7... | collective-permute-start | bytes 98312 | tf_op jit(solution)/shard_map/while/body/eval_jaxpr/ppermute | solution.py:16
  334.8 5.1 collective-permute-start.1
  340.0 8.3 %collective-permute-start = (bf16[1,128,128]{2,1,0:T(8,128)(2,1)S(1)}, bf16[1,128,128]{2,1,0:T(8,128)(2,1)S(1)}, u32[]{:S(2)}, u32[]{:S(2)}) collective-permute-start(bf16[1,128,128]{2,1,0:T(8,128)(2,1)S(1)} %fusion.74), channel_id=1, source_target_pairs={{0,8},{8,16},{16,24},{24,32},{32,40},{40,48},{48,56},{56,64},{64,7... | collective-permute-start | bytes 98312 | tf_op jit(solution)/shard_map/while/body/eval_jaxpr/ppermute | solution.py:16
  348.3 7.7 %collective-permute-start = (bf16[1,128,128]{2,1,0:T(8,128)(2,1)S(1)}, bf16[1,128,128]{2,1,0:T(8,128)(2,1)S(1)}, u32[]{:S(2)}, u32[]{:S(2)}) collective-permute-start(bf16[1,128,128]{2,1,0:T(8,128)(2,1)S(1)} %fusion.74), channel_id=1, source_target_pairs={{0,8},{8,16},{16,24},{24,32},{32,40},{40,48},{48,56},{56,64},{64,7... | collective-permute-start | bytes 98312 | tf_op jit(solution)/shard_map/while/body/eval_jaxpr/ppermute | solution.py:16
  356.1 8.0 %collective-permute-start = (bf16[1,128,128]{2,1,0:T(8,128)(2,1)S(1)}, bf16[1,128,128]{2,1,0:T(8,128)(2,1)S(1)}, u32[]{:S(2)}, u32[]{:S(2)}) collective-permute-start(bf16[1,128,128]{2,1,0:T(8,128)(2,1)S(1)} %fusion.74), channel_id=1, source_target_pairs={{0,8},{8,16},{16,24},{24,32},{32,40},{40,48},{48,56},{56,64},{64,7... | collective-permute-start | bytes 98312 | tf_op jit(solution)/shard_map/while/body/eval_jaxpr/ppermute | solution.py:16
  364.1 8.6 %collective-permute-start = (bf16[1,128,128]{2,1,0:T(8,128)(2,1)S(1)}, bf16[1,128,128]{2,1,0:T(8,128)(2,1)S(1)}, u32[]{:S(2)}, u32[]{:S(2)}) collective-permute-start(bf16[1,128,128]{2,1,0:T(8,128)(2,1)S(1)} %fusion.74), channel_id=1, source_target_pairs={{0,8},{8,16},{16,24},{24,32},{32,40},{40,48},{48,56},{56,64},{64,7... | collective-permute-start | bytes 98312 | tf_op jit(solution)/shard_map/while/body/eval_jaxpr/ppermute | solution.py:16
  367.7 5.0 collective-permute-start.1
  372.8 8.2 %collective-permute-start = (bf16[1,128,128]{2,1,0:T(8,128)(2,1)S(1)}, bf16[1,128,128]{2,1,0:T(8,128)(2,1)S(1)}, u32[]{:S(2)}, u32[]{:S(2)}) collective-permute-start(bf16[1,128,128]{2,1,0:T(8,128)(2,1)S(1)} %fusion.74), channel_id=1, source_target_pairs={{0,8},{8,16},{16,24},{24,32},{32,40},{40,48},{48,56},{56,64},{64,7... | collective-permute-start | bytes 98312 | tf_op jit(solution)/shard_map/while/body/eval_jaxpr/ppermute | solution.py:16
  381.0 8.4 %collective-permute-start = (bf16[1,128,128]{2,1,0:T(8,128)(2,1)S(1)}, bf16[1,128,128]{2,1,0:T(8,128)(2,1)S(1)}, u32[]{:S(2)}, u32[]{:S(2)}) collective-permute-start(bf16[1,128,128]{2,1,0:T(8,128)(2,1)S(1)} %fusion.74), channel_id=1, source_target_pairs={{0,8},{8,16},{16,24},{24,32},{32,40},{40,48},{48,56},{56,64},{64,7... | collective-permute-start | bytes 98312 | tf_op jit(solution)/shard_map/while/body/eval_jaxpr/ppermute | solution.py:16
  384.6 4.8 collective-permute-start.1
  389.5 8.2 %collective-permute-start = (bf16[1,128,128]{2,1,0:T(8,128)(2,1)S(1)}, bf16[1,128,128]{2,1,0:T(8,128)(2,1)S(1)}, u32[]{:S(2)}, u32[]{:S(2)}) collective-permute-start(bf16[1,128,128]{2,1,0:T(8,128)(2,1)S(1)} %fusion.74), channel_id=1, source_target_pairs={{0,8},{8,16},{16,24},{24,32},{32,40},{40,48},{48,56},{56,64},{64,7... | collective-permute-start | bytes 98312 | tf_op jit(solution)/shard_map/while/body/eval_jaxpr/ppermute | solution.py:16
  397.8 8.3 %collective-permute-start = (bf16[1,128,128]{2,1,0:T(8,128)(2,1)S(1)}, bf16[1,128,128]{2,1,0:T(8,128)(2,1)S(1)}, u32[]{:S(2)}, u32[]{:S(2)}) collective-permute-start(bf16[1,128,128]{2,1,0:T(8,128)(2,1)S(1)} %fusion.74), channel_id=1, source_target_pairs={{0,8},{8,16},{16,24},{24,32},{32,40},{40,48},{48,56},{56,64},{64,7... | collective-permute-start | bytes 98312 | tf_op jit(solution)/shard_map/while/body/eval_jaxpr/ppermute | solution.py:16
  401.3 4.7 collective-permute-start.1
  406.1 8.3 %collective-permute-start = (bf16[1,128,128]{2,1,0:T(8,128)(2,1)S(1)}, bf16[1,128,128]{2,1,0:T(8,128)(2,1)S(1)}, u32[]{:S(2)}, u32[]{:S(2)}) collective-permute-start(bf16[1,128,128]{2,1,0:T(8,128)(2,1)S(1)} %fusion.74), channel_id=1, source_target_pairs={{0,8},{8,16},{16,24},{24,32},{32,40},{40,48},{48,56},{56,64},{64,7... | collective-permute-start | bytes 98312 | tf_op jit(solution)/shard_map/while/body/eval_jaxpr/ppermute | solution.py:16
  409.7 4.7 collective-permute-start.1
  414.5 8.3 %collective-permute-start = (bf16[1,128,128]{2,1,0:T(8,128)(2,1)S(1)}, bf16[1,128,128]{2,1,0:T(8,128)(2,1)S(1)}, u32[]{:S(2)}, u32[]{:S(2)}) collective-permute-start(bf16[1,128,128]{2,1,0:T(8,128)(2,1)S(1)} %fusion.74), channel_id=1, source_target_pairs={{0,8},{8,16},{16,24},{24,32},{32,40},{40,48},{48,56},{56,64},{64,7... | collective-permute-start | bytes 98312 | tf_op jit(solution)/shard_map/while/body/eval_jaxpr/ppermute | solution.py:16
  418.1 4.7 collective-permute-start.1
  (28 other events, 1103.5 us)
Sparse Core Ops, SparseCore 0:
  10.0 75.5 all-gather.4
  88.2 73.7 all-gather.6
  164.6 81.8 all-gather.8
  248.8 82.8 all-gather.10
  454.6 97.9 reduce-scatter.1
where the time goes:
time: 565 us; the launch traced here: 559 us
  waiting for transfers between devices  253 us (45%)
  starting transfers between devices  230 us (41%)
  matrix products  40.5 us (7%)
  other arithmetic  19.2 us (3%)
  between operations  13.4 us (2%)
    ppermute x62, starting transfers between devices, from_behind(): return lax.ppermute(block, axis, route)  230 us
    reduce_scatter x1, waiting for transfers between devices, per_device(): lax.psum_scatter(partial_out.astype(jnp.bfloat16), 'head', scatter_dimens...  98.1 us
    all_gather x1, waiting for transfers between devices, per_device(): value_wide = project(lax.all_gather(wv, 'seq', axis=0, tiled=True))  70.3 us
    all_gather x1, waiting for transfers between devices, per_device(): key_wide = project(lax.all_gather(wk, 'seq', axis=0, tiled=True))  60.1 us
    ppermute x62, waiting for transfers between devices, from_behind(): return lax.ppermute(block, axis, route)  21.9 us
    dot_general x3, matrix products, project(): return jnp.dot(normed, shard_piece, preferred_element_type=jnp.float32)  20.9 us
  transfers between devices with their start and end apart: 67, of which 34 were waited for; matrix products, arithmetic and copies ran while one was open for 9% of the time, Pallas kernels for 0%

commit v1 on v0

--- a/solution.py
+++ b/solution.py
@@ -8,6 +8,12 @@
 KVH = 8
 HD = 128
 SEG = 512
+
+
+def tiled_gather(x, axis, dim):
+    peers = lax.axis_size(axis)
+    repeats = [peers if d == dim else 1 for d in range(x.ndim)]
+    return lax.all_to_all(jnp.tile(x, repeats), axis, split_axis=dim, concat_axis=dim, tiled=True)
 
 
 def from_behind(block, axis, distance):
@@ -32,7 +38,7 @@
         return jnp.dot(normed, shard_piece, preferred_element_type=jnp.float32)
 
     query_wide = project(lax.all_gather(wq, "seq", axis=0, tiled=True))
-    key_wide = project(lax.all_gather(wk, "seq", axis=0, tiled=True))
+    key_wide = project(tiled_gather(wk, "seq", 0))
     value_wide = project(lax.all_gather(wv, "seq", axis=0, tiled=True))
     queries = query_wide.astype(jnp.bfloat16)
     keys_all = key_wide.astype(jnp.bfloat16)

time: 565 us -> 490 us (0.87)
  waiting for transfers between devices: 253 us -> 164 us
  starting transfers between devices: 230 us -> 242 us
    all_gather x1 -> x0, waiting for transfers between devices: 60.1 us -> none  [per_device(): key_wide = project(lax.all_gather(wk, 'seq', axis=0, tiled=True))]
    all_gather x1, waiting for transfers between devices: 70.3 us -> 33.1 us  [per_device(): value_wide = project(lax.all_gather(wv, 'seq', axis=0, tiled=True))]
    all_to_all x0 -> x1, starting transfers between devices: none -> 12 us  [tiled_gather(): lax.all_to_all(jnp.tile(x, repeats), axis, split_axis=dim, concat_axis=di...]
    all_to_all x0 -> x1, waiting for transfers between devices: none -> 8.47 us  [tiled_gather(): lax.all_to_all(jnp.tile(x, repeats), axis, split_axis=dim, concat_axis=di...]
  transfers between devices with their start and end apart: 67 -> 67, of which waited for: 34 -> 34; matrix products, arithmetic and copies ran while one was open for 9% -> 11% of each run, Pallas kernels for 0% -> 0%
where the time goes in v1:
time: 490 us; the launch traced here: 484 us
  starting transfers between devices  242 us (49%)
  waiting for transfers between devices  164 us (33%)
  matrix products  40.3 us (8%)
  other arithmetic  19.9 us (4%)
  between operations  13.4 us (3%)
    ppermute x62, starting transfers between devices, from_behind(): return lax.ppermute(block, axis, route)  230 us
    reduce_scatter x1, waiting for transfers between devices, per_device(): lax.psum_scatter(partial_out.astype(jnp.bfloat16), 'head', scatter_dimens...  98.1 us
    all_gather x1, waiting for transfers between devices, per_device(): value_wide = project(lax.all_gather(wv, 'seq', axis=0, tiled=True))  33.1 us
    ppermute x62, waiting for transfers between devices, from_behind(): return lax.ppermute(block, axis, route)  21.9 us
    dot_general x3, matrix products, project(): return jnp.dot(normed, shard_piece, preferred_element_type=jnp.float32)  20.7 us
    all_to_all x1, starting transfers between devices, tiled_gather(): lax.all_to_all(jnp.tile(x, repeats), axis, split_axis=dim, concat_axis=di...  12 us
    convert_element_type x1, other arithmetic, per_device(): normed = (widened * lax.rsqrt(jnp.mean(widened * widened, axis=-1, keepdi...  10.3 us
  transfers between devices with their start and end apart: 67, of which 34 were waited for; matrix products, arithmetic and copies ran while one was open for 11% of the time, Pallas kernels for 0%

profile of v1, /device:TPU:1, one launch (start us, length us, event | category | flops | bytes accessed | tf_op | source)
XLA Modules:
  0.0 484.2 jit_solution(9521950406188183402)
XLA Ops:
  10.0 12.0 %all-to-all-start = ((bf16[32,128,128]{2,1,0:T(8,128)(2,1)}), bf16[32,128,128]{2,1,0:T(8,128)(2,1)S(1)}, u32[]{:S(2)}, u32[]{:S(2)}) async-start(bf16[32,128,128]{2,1,0:T(8,128)(2,1)} %tile.2), calls=%async_computation | async-start | bytes 2097152 | tf_op jit(solution)/shard_map/all_to_all | solution.py:16
  24.2 5.1 %fusion.3 = f32[1024]{0:T(1024)S(1)} fusion(bf16[1024,4096]{1,0:T(8,128)(2,1)} %param.11), kind=kLoop, calls=%fused_computation.7 | loop fusion | flops 12581888 | bytes 8392704 | tf_op jit(solution)/shard_map/reduce_sum | solution.py:33
  29.3 10.3 %fusion.5 = bf16[1024,4096]{1,0:T(8,128)(2,1)} fusion(bf16[1024,4096]{1,0:T(8,128)(2,1)} %param.11, f32[4096]{0:T(1024)S(1)} %copy-done.2, f32[1024]{0:T(1024)S(1)} %add_rsqrt_fusion), kind=kLoop, calls=%fused_computation.9 | loop fusion | flops 16777216 | bytes 16797696 | tf_op jit(solution)/shard_map/convert_element_type | solution.py:34
  39.6 8.5 %all-to-all-done = bf16[32,128,128]{2,1,0:T(8,128)(2,1)S(1)} async-done(((bf16[32,128,128]{2,1,0:T(8,128)(2,1)}), bf16[32,128,128]{2,1,0:T(8,128)(2,1)S(1)}, u32[]{:S(2)}, u32[]{:S(2)}) %all-to-all-start) | async-done | bytes 1048608 | tf_op jit(solution)/shard_map/all_to_all | solution.py:16
  48.1 5.7 %fusion.38 = (f32[128]{0:T(128)S(1)}, bf16[1024,128]{1,0:T(8,128)(2,1)S(1)}) fusion(bf16[1024,4096]{1,0:T(8,128)(2,1)} %fusion.5, bf16[4096,128]{1,0:T(8,128)(2,1)S(1)} %bitcast.94), kind=kOutput, calls=%fused_computation.57 | convolution fusion | flops 1074659200 | bytes 9699840 | tf_op jit(solution)/shard_map/dot_general | solution.py:38
  54.0 33.1 %all-gather.4.cloned.1.call-done = bf16[4096,128]{1,0:T(8,128)(2,1)} async-done(((bf16[128,128]{1,0:T(8,128)(2,1)}), bf16[4096,128]{1,0:T(8,128)(2,1)}) %all-gather.4.cloned.1.call-update) | async-done | bytes 1048592 | tf_op jit(solution)/shard_map/all_gather | solution.py:42
  87.1 5.9 %convolution_convert_fusion.2 = bf16[1024,128]{1,0:T(8,128)(2,1)S(1)} fusion(bf16[1024,4096]{1,0:T(8,128)(2,1)} %fusion.5, bf16[4096,128]{1,0:T(8,128)(2,1)} %all-gather.4.cloned.1.call-done), kind=kOutput, calls=%fused_computation.32 | convolution fusion | flops 1073872896 | bytes 9699328 | tf_op jit(solution)/shard_map/dot_general | solution.py:38
  94.0 254.0 %while.13 = (s32[]{:T(128)}, f32[1,128,128]{2,1,0:T(8,128)S(1)}, f32[1,128]{1,0:T(1,128)S(1)}, f32[1,128,128]{2,1,0:T(8,128)S(1)}, f32[1,128]{1,0:T(1,128)S(1)}, /*index=5*/s32[]{:T(128)}, s32[]{:T(128)}) while((s32[]{:T(128)}, f32[1,128,128]{2,1,0:T(8,128)S(1)}, f32[1,128]{1,0:T(1,128)S(1)}, f32[1,128,128]{2,1,0:T(8,128)S(1)}, ...), condition=%wide.region_4.5_spmd.clone, body=%wide.region_3.4_spmd.clone.sunk | while | flops 66051 | bytes 396456 | solution.py:68
  96.3 4.0 collective-permute-start.1
  107.3 4.0 collective-permute-start
  115.4 4.0 collective-permute-start
  122.9 4.0 collective-permute-start
  138.9 3.7 collective-permute-start
  146.4 4.0 collective-permute-start
  150.4 3.8 collective-permute-start.1
  154.9 4.0 collective-permute-start
  158.9 4.0 collective-permute-start.1
  163.7 4.0 collective-permute-start
  172.0 4.0 collective-permute-start
  176.0 3.6 collective-permute-start.1
  180.3 3.7 collective-permute-start
  184.0 4.0 collective-permute-start.1
  188.7 3.9 collective-permute-start
  192.6 3.7 collective-permute-start.1
  205.0 3.9 collective-permute-start
  208.9 4.0 collective-permute-start.1
  213.6 3.7 collective-permute-start
  217.4 3.9 collective-permute-start.1
  222.0 3.6 collective-permute-start
  225.6 4.0 collective-permute-start.1
  230.4 4.0 collective-permute-start
  234.4 4.1 collective-permute-start.1
  239.2 4.0 collective-permute-start
  243.2 4.0 collective-permute-start.1
  248.0 4.0 collective-permute-start
  259.6 4.8 collective-permute-start.1
  265.1 3.9 collective-permute-start
  284.8 3.7 collective-permute-start.1
  292.9 4.3 collective-permute-start.1
  298.0 3.9 collective-permute-start
  309.8 4.1 collective-permute-start.1
  318.2 3.9 collective-permute-start.1
  326.5 4.0 collective-permute-start.1
  334.8 4.0 collective-permute-start.1
  343.2 4.0 collective-permute-start.1
  348.1 9.1 %convolution_convert_fusion.1 = bf16[1024,512]{1,0:T(8,128)(2,1)S(1)} fusion(bf16[1024,4096]{1,0:T(8,128)(2,1)} %fusion.5, bf16[4096,512]{1,0:T(8,128)(2,1)} %all-gather.6.cloned.1.call-done), kind=kOutput, calls=%fused_computation.31 | convolution fusion | flops 4295491584 | bytes 13631488 | tf_op jit(solution)/shard_map/dot_general | solution.py:38
  370.7 8.9 %convolution_convert_fusion = bf16[1024,4096]{1,0:T(8,128)(2,1)} fusion(bf16[512,4096]{1,0:T(8,128)(2,1)} %all-gather.8.cloned.1.call-done, bf16[128,8,4,128]{3,2,1,0:T(4,128)(2,1)S(1)} %bitcast.95), kind=kOutput, calls=%fused_computation.13 | convolution fusion | flops 4299161600 | bytes 13631488 | tf_op jit(solution)/shard_map/dot_general | solution.py:98
  379.6 98.1 %reduce-scatter.2.cloned.1.call-done = bf16[1024,512]{1,0:T(8,128)(2,1)} async-done(((bf16[1024,4096]{1,0:T(8,128)(2,1)}), bf16[1024,512]{1,0:T(8,128)(2,1)}) %reduce-scatter.2.cloned.1.call-update) | async-done | bytes 1048592 | tf_op jit(solution)/shard_map/reduce_scatter | solution.py:101
  (259 shorter events, 126.8 us)
Async XLA Ops:
  6.5 80.6 %all-gather.4.cloned.1.call-start = ((), (), s32[]{:S(2)}) async-start(), calls=%async_computation.2 | async-start | bytes 1081344 | tf_op jit(solution)/shard_map/all_gather | solution.py:42
  7.3 340.8 %all-gather.6.cloned.1.call-start = ((), (), s32[]{:S(2)}) async-start(), calls=%async_computation.3 | async-start | bytes 4325376 | tf_op jit(solution)/shard_map/all_gather | solution.py:40
  10.0 38.1 %all-to-all-start = ((bf16[32,128,128]{2,1,0:T(8,128)(2,1)}), bf16[32,128,128]{2,1,0:T(8,128)(2,1)S(1)}, u32[]{:S(2)}, u32[]{:S(2)}) async-start(bf16[32,128,128]{2,1,0:T(8,128)(2,1)} %tile.2), calls=%async_computation | async-start | bytes 2097152 | tf_op jit(solution)/shard_map/all_to_all | solution.py:16
  22.0 348.7 %all-gather.8.cloned.1.call-start = ((), (), s32[]{:S(2)}) async-start(), calls=%async_computation.4 | async-start | bytes 4325376 | tf_op jit(solution)/shard_map/all_gather | solution.py:99
  22.8 455.0 %reduce-scatter.2.cloned.1.call-start = ((), (), s32[]{:S(2)}) async-start(), calls=%async_computation.5 | async-start | bytes 9437184 | tf_op jit(solution)/shard_map/reduce_scatter | solution.py:101
  94.0 6.9 %collective-permute-start = (bf16[1,128,128]{2,1,0:T(8,128)(2,1)S(1)}, bf16[1,128,128]{2,1,0:T(8,128)(2,1)S(1)}, u32[]{:S(2)}, u32[]{:S(2)}) collective-permute-start(bf16[1,128,128]{2,1,0:T(8,128)(2,1)S(1)} %fusion.74), channel_id=1, source_target_pairs={{0,8},{8,16},{16,24},{24,32},{32,40},{40,48},{48,56},{56,64},{64,7... | collective-permute-start | bytes 98312 | tf_op jit(solution)/shard_map/while/body/eval_jaxpr/ppermute | solution.py:22
  96.3 4.7 collective-permute-start.1
  101.0 6.2 %collective-permute-start = (bf16[1,128,128]{2,1,0:T(8,128)(2,1)S(1)}, bf16[1,128,128]{2,1,0:T(8,128)(2,1)S(1)}, u32[]{:S(2)}, u32[]{:S(2)}) collective-permute-start(bf16[1,128,128]{2,1,0:T(8,128)(2,1)S(1)} %fusion.74), channel_id=1, source_target_pairs={{0,8},{8,16},{16,24},{24,32},{32,40},{40,48},{48,56},{56,64},{64,7... | collective-permute-start | bytes 98312 | tf_op jit(solution)/shard_map/while/body/eval_jaxpr/ppermute | solution.py:22
  107.3 8.1 %collective-permute-start = (bf16[1,128,128]{2,1,0:T(8,128)(2,1)S(1)}, bf16[1,128,128]{2,1,0:T(8,128)(2,1)S(1)}, u32[]{:S(2)}, u32[]{:S(2)}) collective-permute-start(bf16[1,128,128]{2,1,0:T(8,128)(2,1)S(1)} %fusion.74), channel_id=1, source_target_pairs={{0,8},{8,16},{16,24},{24,32},{32,40},{40,48},{48,56},{56,64},{64,7... | collective-permute-start | bytes 98312 | tf_op jit(solution)/shard_map/while/body/eval_jaxpr/ppermute | solution.py:22
  115.4 7.4 %collective-permute-start = (bf16[1,128,128]{2,1,0:T(8,128)(2,1)S(1)}, bf16[1,128,128]{2,1,0:T(8,128)(2,1)S(1)}, u32[]{:S(2)}, u32[]{:S(2)}) collective-permute-start(bf16[1,128,128]{2,1,0:T(8,128)(2,1)S(1)} %fusion.74), channel_id=1, source_target_pairs={{0,8},{8,16},{16,24},{24,32},{32,40},{40,48},{48,56},{56,64},{64,7... | collective-permute-start | bytes 98312 | tf_op jit(solution)/shard_map/while/body/eval_jaxpr/ppermute | solution.py:22
  122.9 8.1 %collective-permute-start = (bf16[1,128,128]{2,1,0:T(8,128)(2,1)S(1)}, bf16[1,128,128]{2,1,0:T(8,128)(2,1)S(1)}, u32[]{:S(2)}, u32[]{:S(2)}) collective-permute-start(bf16[1,128,128]{2,1,0:T(8,128)(2,1)S(1)} %fusion.74), channel_id=1, source_target_pairs={{0,8},{8,16},{16,24},{24,32},{32,40},{40,48},{48,56},{56,64},{64,7... | collective-permute-start | bytes 98312 | tf_op jit(solution)/shard_map/while/body/eval_jaxpr/ppermute | solution.py:22
  131.0 7.8 %collective-permute-start = (bf16[1,128,128]{2,1,0:T(8,128)(2,1)S(1)}, bf16[1,128,128]{2,1,0:T(8,128)(2,1)S(1)}, u32[]{:S(2)}, u32[]{:S(2)}) collective-permute-start(bf16[1,128,128]{2,1,0:T(8,128)(2,1)S(1)} %fusion.74), channel_id=1, source_target_pairs={{0,8},{8,16},{16,24},{24,32},{32,40},{40,48},{48,56},{56,64},{64,7... | collective-permute-start | bytes 98312 | tf_op jit(solution)/shard_map/while/body/eval_jaxpr/ppermute | solution.py:22
  138.9 7.4 %collective-permute-start = (bf16[1,128,128]{2,1,0:T(8,128)(2,1)S(1)}, bf16[1,128,128]{2,1,0:T(8,128)(2,1)S(1)}, u32[]{:S(2)}, u32[]{:S(2)}) collective-permute-start(bf16[1,128,128]{2,1,0:T(8,128)(2,1)S(1)} %fusion.74), channel_id=1, source_target_pairs={{0,8},{8,16},{16,24},{24,32},{32,40},{40,48},{48,56},{56,64},{64,7... | collective-permute-start | bytes 98312 | tf_op jit(solution)/shard_map/while/body/eval_jaxpr/ppermute | solution.py:22
  146.4 8.5 %collective-permute-start = (bf16[1,128,128]{2,1,0:T(8,128)(2,1)S(1)}, bf16[1,128,128]{2,1,0:T(8,128)(2,1)S(1)}, u32[]{:S(2)}, u32[]{:S(2)}) collective-permute-start(bf16[1,128,128]{2,1,0:T(8,128)(2,1)S(1)} %fusion.74), channel_id=1, source_target_pairs={{0,8},{8,16},{16,24},{24,32},{32,40},{40,48},{48,56},{56,64},{64,7... | collective-permute-start | bytes 98312 | tf_op jit(solution)/shard_map/while/body/eval_jaxpr/ppermute | solution.py:22
  154.9 8.7 %collective-permute-start = (bf16[1,128,128]{2,1,0:T(8,128)(2,1)S(1)}, bf16[1,128,128]{2,1,0:T(8,128)(2,1)S(1)}, u32[]{:S(2)}, u32[]{:S(2)}) collective-permute-start(bf16[1,128,128]{2,1,0:T(8,128)(2,1)S(1)} %fusion.74), channel_id=1, source_target_pairs={{0,8},{8,16},{16,24},{24,32},{32,40},{40,48},{48,56},{56,64},{64,7... | collective-permute-start | bytes 98312 | tf_op jit(solution)/shard_map/while/body/eval_jaxpr/ppermute | solution.py:22
  158.9 4.7 collective-permute-start.1
  163.7 8.3 %collective-permute-start = (bf16[1,128,128]{2,1,0:T(8,128)(2,1)S(1)}, bf16[1,128,128]{2,1,0:T(8,128)(2,1)S(1)}, u32[]{:S(2)}, u32[]{:S(2)}) collective-permute-start(bf16[1,128,128]{2,1,0:T(8,128)(2,1)S(1)} %fusion.74), channel_id=1, source_target_pairs={{0,8},{8,16},{16,24},{24,32},{32,40},{40,48},{48,56},{56,64},{64,7... | collective-permute-start | bytes 98312 | tf_op jit(solution)/shard_map/while/body/eval_jaxpr/ppermute | solution.py:22
  172.0 8.3 %collective-permute-start = (bf16[1,128,128]{2,1,0:T(8,128)(2,1)S(1)}, bf16[1,128,128]{2,1,0:T(8,128)(2,1)S(1)}, u32[]{:S(2)}, u32[]{:S(2)}) collective-permute-start(bf16[1,128,128]{2,1,0:T(8,128)(2,1)S(1)} %fusion.74), channel_id=1, source_target_pairs={{0,8},{8,16},{16,24},{24,32},{32,40},{40,48},{48,56},{56,64},{64,7... | collective-permute-start | bytes 98312 | tf_op jit(solution)/shard_map/while/body/eval_jaxpr/ppermute | solution.py:22
  180.3 8.4 %collective-permute-start = (bf16[1,128,128]{2,1,0:T(8,128)(2,1)S(1)}, bf16[1,128,128]{2,1,0:T(8,128)(2,1)S(1)}, u32[]{:S(2)}, u32[]{:S(2)}) collective-permute-start(bf16[1,128,128]{2,1,0:T(8,128)(2,1)S(1)} %fusion.74), channel_id=1, source_target_pairs={{0,8},{8,16},{16,24},{24,32},{32,40},{40,48},{48,56},{56,64},{64,7... | collective-permute-start | bytes 98312 | tf_op jit(solution)/shard_map/while/body/eval_jaxpr/ppermute | solution.py:22
  188.7 8.3 %collective-permute-start = (bf16[1,128,128]{2,1,0:T(8,128)(2,1)S(1)}, bf16[1,128,128]{2,1,0:T(8,128)(2,1)S(1)}, u32[]{:S(2)}, u32[]{:S(2)}) collective-permute-start(bf16[1,128,128]{2,1,0:T(8,128)(2,1)S(1)} %fusion.74), channel_id=1, source_target_pairs={{0,8},{8,16},{16,24},{24,32},{32,40},{40,48},{48,56},{56,64},{64,7... | collective-permute-start | bytes 98312 | tf_op jit(solution)/shard_map/while/body/eval_jaxpr/ppermute | solution.py:22
  197.1 7.9 %collective-permute-start = (bf16[1,128,128]{2,1,0:T(8,128)(2,1)S(1)}, bf16[1,128,128]{2,1,0:T(8,128)(2,1)S(1)}, u32[]{:S(2)}, u32[]{:S(2)}) collective-permute-start(bf16[1,128,128]{2,1,0:T(8,128)(2,1)S(1)} %fusion.74), channel_id=1, source_target_pairs={{0,8},{8,16},{16,24},{24,32},{32,40},{40,48},{48,56},{56,64},{64,7... | collective-permute-start | bytes 98312 | tf_op jit(solution)/shard_map/while/body/eval_jaxpr/ppermute | solution.py:22
  205.0 8.6 %collective-permute-start = (bf16[1,128,128]{2,1,0:T(8,128)(2,1)S(1)}, bf16[1,128,128]{2,1,0:T(8,128)(2,1)S(1)}, u32[]{:S(2)}, u32[]{:S(2)}) collective-permute-start(bf16[1,128,128]{2,1,0:T(8,128)(2,1)S(1)} %fusion.74), channel_id=1, source_target_pairs={{0,8},{8,16},{16,24},{24,32},{32,40},{40,48},{48,56},{56,64},{64,7... | collective-permute-start | bytes 98312 | tf_op jit(solution)/shard_map/while/body/eval_jaxpr/ppermute | solution.py:22
  208.9 4.7 collective-permute-start.1
  213.6 8.3 %collective-permute-start = (bf16[1,128,128]{2,1,0:T(8,128)(2,1)S(1)}, bf16[1,128,128]{2,1,0:T(8,128)(2,1)S(1)}, u32[]{:S(2)}, u32[]{:S(2)}) collective-permute-start(bf16[1,128,128]{2,1,0:T(8,128)(2,1)S(1)} %fusion.74), channel_id=1, source_target_pairs={{0,8},{8,16},{16,24},{24,32},{32,40},{40,48},{48,56},{56,64},{64,7... | collective-permute-start | bytes 98312 | tf_op jit(solution)/shard_map/while/body/eval_jaxpr/ppermute | solution.py:22
  222.0 8.4 %collective-permute-start = (bf16[1,128,128]{2,1,0:T(8,128)(2,1)S(1)}, bf16[1,128,128]{2,1,0:T(8,128)(2,1)S(1)}, u32[]{:S(2)}, u32[]{:S(2)}) collective-permute-start(bf16[1,128,128]{2,1,0:T(8,128)(2,1)S(1)} %fusion.74), channel_id=1, source_target_pairs={{0,8},{8,16},{16,24},{24,32},{32,40},{40,48},{48,56},{56,64},{64,7... | collective-permute-start | bytes 98312 | tf_op jit(solution)/shard_map/while/body/eval_jaxpr/ppermute | solution.py:22
  225.6 4.7 collective-permute-start.1
  230.4 8.8 %collective-permute-start = (bf16[1,128,128]{2,1,0:T(8,128)(2,1)S(1)}, bf16[1,128,128]{2,1,0:T(8,128)(2,1)S(1)}, u32[]{:S(2)}, u32[]{:S(2)}) collective-permute-start(bf16[1,128,128]{2,1,0:T(8,128)(2,1)S(1)} %fusion.74), channel_id=1, source_target_pairs={{0,8},{8,16},{16,24},{24,32},{32,40},{40,48},{48,56},{56,64},{64,7... | collective-permute-start | bytes 98312 | tf_op jit(solution)/shard_map/while/body/eval_jaxpr/ppermute | solution.py:22
  234.4 4.8 collective-permute-start.1
  239.2 8.7 %collective-permute-start = (bf16[1,128,128]{2,1,0:T(8,128)(2,1)S(1)}, bf16[1,128,128]{2,1,0:T(8,128)(2,1)S(1)}, u32[]{:S(2)}, u32[]{:S(2)}) collective-permute-start(bf16[1,128,128]{2,1,0:T(8,128)(2,1)S(1)} %fusion.74), channel_id=1, source_target_pairs={{0,8},{8,16},{16,24},{24,32},{32,40},{40,48},{48,56},{56,64},{64,7... | collective-permute-start | bytes 98312 | tf_op jit(solution)/shard_map/while/body/eval_jaxpr/ppermute | solution.py:22
  243.2 4.7 collective-permute-start.1
  248.0 8.0 %collective-permute-start = (bf16[1,128,128]{2,1,0:T(8,128)(2,1)S(1)}, bf16[1,128,128]{2,1,0:T(8,128)(2,1)S(1)}, u32[]{:S(2)}, u32[]{:S(2)}) collective-permute-start(bf16[1,128,128]{2,1,0:T(8,128)(2,1)S(1)} %fusion.74), channel_id=1, source_target_pairs={{0,8},{8,16},{16,24},{24,32},{32,40},{40,48},{48,56},{56,64},{64,7... | collective-permute-start | bytes 98312 | tf_op jit(solution)/shard_map/while/body/eval_jaxpr/ppermute | solution.py:22
  256.0 9.1 %collective-permute-start = (bf16[1,128,128]{2,1,0:T(8,128)(2,1)S(1)}, bf16[1,128,128]{2,1,0:T(8,128)(2,1)S(1)}, u32[]{:S(2)}, u32[]{:S(2)}) collective-permute-start(bf16[1,128,128]{2,1,0:T(8,128)(2,1)S(1)} %fusion.74), channel_id=1, source_target_pairs={{0,8},{8,16},{16,24},{24,32},{32,40},{40,48},{48,56},{56,64},{64,7... | collective-permute-start | bytes 98312 | tf_op jit(solution)/shard_map/while/body/eval_jaxpr/ppermute | solution.py:22
  259.6 5.5 %collective-permute-start.1 = (bf16[1,128]{1,0:T(2,128)(2,1)S(1)}, bf16[1,128]{1,0:T(2,128)(2,1)S(1)}, u32[]{:S(2)}, u32[]{:S(2)}) collective-permute-start(bf16[1,128]{1,0:T(2,128)(2,1)S(1)} %fusion.75), channel_id=1, source_target_pairs={{0,8},{8,16},{16,24},{24,32},{32,40},{40,48},{48,56},{56,64},{64,7... | collective-permute-start | bytes 776 | tf_op jit(solution)/shard_map/while/body/eval_jaxpr/ppermute | solution.py:22
  265.1 8.2 %collective-permute-start = (bf16[1,128,128]{2,1,0:T(8,128)(2,1)S(1)}, bf16[1,128,128]{2,1,0:T(8,128)(2,1)S(1)}, u32[]{:S(2)}, u32[]{:S(2)}) collective-permute-start(bf16[1,128,128]{2,1,0:T(8,128)(2,1)S(1)} %fusion.74), channel_id=1, source_target_pairs={{0,8},{8,16},{16,24},{24,32},{32,40},{40,48},{48,56},{56,64},{64,7... | collective-permute-start | bytes 98312 | tf_op jit(solution)/shard_map/while/body/eval_jaxpr/ppermute | solution.py:22
  273.4 7.8 %collective-permute-start = (bf16[1,128,128]{2,1,0:T(8,128)(2,1)S(1)}, bf16[1,128,128]{2,1,0:T(8,128)(2,1)S(1)}, u32[]{:S(2)}, u32[]{:S(2)}) collective-permute-start(bf16[1,128,128]{2,1,0:T(8,128)(2,1)S(1)} %fusion.74), channel_id=1, source_target_pairs={{0,8},{8,16},{16,24},{24,32},{32,40},{40,48},{48,56},{56,64},{64,7... | collective-permute-start | bytes 98312 | tf_op jit(solution)/shard_map/while/body/eval_jaxpr/ppermute | solution.py:22
  281.2 8.0 %collective-permute-start = (bf16[1,128,128]{2,1,0:T(8,128)(2,1)S(1)}, bf16[1,128,128]{2,1,0:T(8,128)(2,1)S(1)}, u32[]{:S(2)}, u32[]{:S(2)}) collective-permute-start(bf16[1,128,128]{2,1,0:T(8,128)(2,1)S(1)} %fusion.74), channel_id=1, source_target_pairs={{0,8},{8,16},{16,24},{24,32},{32,40},{40,48},{48,56},{56,64},{64,7... | collective-permute-start | bytes 98312 | tf_op jit(solution)/shard_map/while/body/eval_jaxpr/ppermute | solution.py:22
  289.3 8.6 %collective-permute-start = (bf16[1,128,128]{2,1,0:T(8,128)(2,1)S(1)}, bf16[1,128,128]{2,1,0:T(8,128)(2,1)S(1)}, u32[]{:S(2)}, u32[]{:S(2)}) collective-permute-start(bf16[1,128,128]{2,1,0:T(8,128)(2,1)S(1)} %fusion.74), channel_id=1, source_target_pairs={{0,8},{8,16},{16,24},{24,32},{32,40},{40,48},{48,56},{56,64},{64,7... | collective-permute-start | bytes 98312 | tf_op jit(solution)/shard_map/while/body/eval_jaxpr/ppermute | solution.py:22
  292.9 5.0 %collective-permute-start.1 = (bf16[1,128]{1,0:T(2,128)(2,1)S(1)}, bf16[1,128]{1,0:T(2,128)(2,1)S(1)}, u32[]{:S(2)}, u32[]{:S(2)}) collective-permute-start(bf16[1,128]{1,0:T(2,128)(2,1)S(1)} %fusion.75), channel_id=1, source_target_pairs={{0,8},{8,16},{16,24},{24,32},{32,40},{40,48},{48,56},{56,64},{64,7... | collective-permute-start | bytes 776 | tf_op jit(solution)/shard_map/while/body/eval_jaxpr/ppermute | solution.py:22
  298.0 8.2 %collective-permute-start = (bf16[1,128,128]{2,1,0:T(8,128)(2,1)S(1)}, bf16[1,128,128]{2,1,0:T(8,128)(2,1)S(1)}, u32[]{:S(2)}, u32[]{:S(2)}) collective-permute-start(bf16[1,128,128]{2,1,0:T(8,128)(2,1)S(1)} %fusion.74), channel_id=1, source_target_pairs={{0,8},{8,16},{16,24},{24,32},{32,40},{40,48},{48,56},{56,64},{64,7... | collective-permute-start | bytes 98312 | tf_op jit(solution)/shard_map/while/body/eval_jaxpr/ppermute | solution.py:22
  306.2 8.4 %collective-permute-start = (bf16[1,128,128]{2,1,0:T(8,128)(2,1)S(1)}, bf16[1,128,128]{2,1,0:T(8,128)(2,1)S(1)}, u32[]{:S(2)}, u32[]{:S(2)}) collective-permute-start(bf16[1,128,128]{2,1,0:T(8,128)(2,1)S(1)} %fusion.74), channel_id=1, source_target_pairs={{0,8},{8,16},{16,24},{24,32},{32,40},{40,48},{48,56},{56,64},{64,7... | collective-permute-start | bytes 98312 | tf_op jit(solution)/shard_map/while/body/eval_jaxpr/ppermute | solution.py:22
  309.8 4.8 collective-permute-start.1
  314.6 8.2 %collective-permute-start = (bf16[1,128,128]{2,1,0:T(8,128)(2,1)S(1)}, bf16[1,128,128]{2,1,0:T(8,128)(2,1)S(1)}, u32[]{:S(2)}, u32[]{:S(2)}) collective-permute-start(bf16[1,128,128]{2,1,0:T(8,128)(2,1)S(1)} %fusion.74), channel_id=1, source_target_pairs={{0,8},{8,16},{16,24},{24,32},{32,40},{40,48},{48,56},{56,64},{64,7... | collective-permute-start | bytes 98312 | tf_op jit(solution)/shard_map/while/body/eval_jaxpr/ppermute | solution.py:22
  322.9 8.3 %collective-permute-start = (bf16[1,128,128]{2,1,0:T(8,128)(2,1)S(1)}, bf16[1,128,128]{2,1,0:T(8,128)(2,1)S(1)}, u32[]{:S(2)}, u32[]{:S(2)}) collective-permute-start(bf16[1,128,128]{2,1,0:T(8,128)(2,1)S(1)} %fusion.74), channel_id=1, source_target_pairs={{0,8},{8,16},{16,24},{24,32},{32,40},{40,48},{48,56},{56,64},{64,7... | collective-permute-start | bytes 98312 | tf_op jit(solution)/shard_map/while/body/eval_jaxpr/ppermute | solution.py:22
  326.5 4.7 collective-permute-start.1
  331.2 8.3 %collective-permute-start = (bf16[1,128,128]{2,1,0:T(8,128)(2,1)S(1)}, bf16[1,128,128]{2,1,0:T(8,128)(2,1)S(1)}, u32[]{:S(2)}, u32[]{:S(2)}) collective-permute-start(bf16[1,128,128]{2,1,0:T(8,128)(2,1)S(1)} %fusion.74), channel_id=1, source_target_pairs={{0,8},{8,16},{16,24},{24,32},{32,40},{40,48},{48,56},{56,64},{64,7... | collective-permute-start | bytes 98312 | tf_op jit(solution)/shard_map/while/body/eval_jaxpr/ppermute | solution.py:22
  334.8 4.7 collective-permute-start.1
  339.6 8.3 %collective-permute-start = (bf16[1,128,128]{2,1,0:T(8,128)(2,1)S(1)}, bf16[1,128,128]{2,1,0:T(8,128)(2,1)S(1)}, u32[]{:S(2)}, u32[]{:S(2)}) collective-permute-start(bf16[1,128,128]{2,1,0:T(8,128)(2,1)S(1)} %fusion.74), channel_id=1, source_target_pairs={{0,8},{8,16},{16,24},{24,32},{32,40},{40,48},{48,56},{56,64},{64,7... | collective-permute-start | bytes 98312 | tf_op jit(solution)/shard_map/while/body/eval_jaxpr/ppermute | solution.py:22
  343.2 4.7 collective-permute-start.1
  (27 other events, 1252.1 us)
Sparse Core Ops, SparseCore 0:
  9.9 77.1 all-gather.3
  89.7 81.8 all-gather.5
  174.1 82.8 all-gather.7
  379.8 97.9 reduce-scatter.1
